TPU v7x, 32 devices: a whole 2x2x4 slice. The times are simulated.
32 devices in a mesh: groups: 2 (over y), blk: 4 (over z), head: 2 (over x), pair: 2 (over core).
Axes of the slice: x: 2, y: 2, z: 4, core: 2. Of those that a mesh axis runs over, the one named last changes fastest.
Arguments:
- single: bfloat16 [256, 384], P(('groups', 'blk')), parts along dimension 0, may hold values from -6 to 6
- pair: bfloat16 [256, 4, 32, 128], P(('groups', 'blk'), None, 'pair'), parts along dimension 0, may hold values from -6 to 6
- frames: float32 [12, 256], P(None, ('groups', 'blk')), parts along dimension 1, as said below
- chain: int32 [256], P(('groups', 'blk')), parts along dimension 0, may hold values from 0 to 5, never falling along the last dimension, each value on 1 to 42 neighbouring positions
- mask: int32 [256], P(('groups', 'blk')), parts along dimension 0, may hold values 0 or 1
- w_query: bfloat16 [384, 192], P(None, 'head'), may hold values from -0.3125 to 0.3125
- w_key_value: bfloat16 [384, 384], P(None, 'head'), may hold values from -0.3125 to 0.3125
- w_query_points: bfloat16 [384, 144], P(None, 'head'), may hold values from -0.3125 to 0.3125
- w_kv_points: bfloat16 [384, 432], P(None, 'head'), may hold values from -0.3125 to 0.3125
- w_pair_bias: bfloat16 [128, 12], P(None, 'head'), may hold values from -0.5 to 0.5
- head_weights: float32 [12], P('head'), may hold values from -9 to 1
- chain_bias: float32 [12], P('head'), may hold values from -3 to 3
- w_out: bfloat16 [12, 176, 384], P('head'), may hold values from -0.125 to 0.125
- out_gain: float32 [384], replicated, may hold values from 0.5 to 1.5
- w_backbone: bfloat16 [384, 6], replicated, may hold values from -0.3125 to 0.3125
Outputs:
- single_out: bfloat16 [256, 384], P(('groups', 'blk')), parts along dimension 0
- frames_out: float32 [12, 256], P(None, 'groups'), parts along dimension 1
There are 2 independent parts, one for each index of `groups`. A program takes and returns all parts, laid end to end along the dimension named above; an argument that names none is the same for every part. Nothing has to cross between parts.
Inputs may be any that keep to these rules, and one draw needn't show every extreme that they name: `frames`: rows 0 to 8 of every column hold an orthonormal rotation matrix row by row; rows 9 to 11 the translation.
All inputs are finite; a program needn't handle non-finite values. No bound on the sum of `mask` on one device may be relied on, other than what follows from the above.
Results may differ from a plain program's by a relative error of at most 0.0048.
Values sent between devices are 32-bit elements; how exact they have to be, the bound alone decides.
A program may use at most 64 MiB of HBM per device.

v0:
```python
import math
import jax
import jax.numpy as jnp
from jax import lax
from jax.sharding import PartitionSpec as P

HIGH = lax.Precision.HIGHEST
LOGIT_WEIGHT = math.sqrt(1.0 / 3.0)
MASK_PENALTY = 100000.0


def shifted(array, axis, by):
    peers = lax.axis_size(axis)
    return lax.ppermute(array, axis, [(i, (i + by) % peers) for i in range(peers)])


def combined_all(value, axis, join):
    pieces = jax.tree.map(lambda part: lax.all_gather(part, axis), value)
    head = jax.tree.map(lambda part: part[0], pieces)
    tail = jax.tree.map(lambda part: part[1:], pieces)
    so_far, _ = lax.scan(lambda so_far, section: (join(so_far, section), None), head, tail)
    return so_far


def to_global(local, frames):
    rotation = frames[:9].reshape(3, 3, -1)
    moved = jnp.einsum("abn,ngb->nga", rotation, local, precision=HIGH)
    return moved + jnp.transpose(frames[9:12])[:, None, :]


def to_local(points, frames):
    rotation = frames[:9].reshape(3, 3, -1)
    moved = points - jnp.transpose(frames[9:12])[:, None, None, :]
    return jnp.einsum("abn,nhpa->nhpb", rotation, moved, precision=HIGH)


def compose(frames, motion):
    rotation = frames[:9].reshape(3, 3, -1)
    inverse = 1.0 / jnp.sqrt(1.0 + motion[:, 0] ** 2 + motion[:, 1] ** 2 + motion[:, 2] ** 2)
    quat_b = motion[:, 0] * inverse
    quat_c = motion[:, 1] * inverse
    quat_d = motion[:, 2] * inverse
    spin = jnp.stack(
        [
            inverse * inverse + quat_b * quat_b - quat_c * quat_c - quat_d * quat_d,
            2.0 * (quat_b * quat_c - inverse * quat_d),
            2.0 * (quat_b * quat_d + inverse * quat_c),
            2.0 * (quat_b * quat_c + inverse * quat_d),
            inverse * inverse - quat_b * quat_b + quat_c * quat_c - quat_d * quat_d,
            2.0 * (quat_c * quat_d - inverse * quat_b),
            2.0 * (quat_b * quat_d - inverse * quat_c),
            2.0 * (quat_c * quat_d + inverse * quat_b),
            inverse * inverse - quat_b * quat_b - quat_c * quat_c + quat_d * quat_d,
        ]
    ).reshape(3, 3, -1)
    new_rotation = jnp.einsum("abn,bcn->acn", rotation, spin, precision=HIGH)
    offset = jnp.einsum("abn,nb->an", rotation, motion[:, 3:6], precision=HIGH)
    return jnp.concatenate([new_rotation.reshape(9, -1), frames[9:12] + offset], axis=0)


def attention_logits(
    pair_rows,
    query_rows,
    query_points,
    query_chain,
    query_present,
    keys,
    key_points,
    key_chain,
    key_present,
    w_pair_bias,
    distance_scale,
    chain_bias,
):
    count_q = pair_rows.shape[0]
    count_k = pair_rows.shape[1]
    bias = jnp.dot(
        pair_rows.reshape(count_q * count_k, -1), w_pair_bias, preferred_element_type=jnp.float32
    ).reshape(count_q, count_k, -1)
    dots = jnp.einsum("ihc,jhc->ijh", query_rows, keys, precision=HIGH) / math.sqrt(keys.shape[-1])
    gaps = query_points[:, None] - key_points[None]
    distance = jnp.sum(gaps * gaps, axis=(3, 4))
    differ = (query_chain[:, None] != key_chain[None, :]).astype(jnp.float32)
    logits = LOGIT_WEIGHT * (
        dots + bias - distance_scale * distance + chain_bias * differ[..., None]
    )
    absent = 1.0 - query_present[:, None] * key_present[None, :]
    return logits - MASK_PENALTY * absent[..., None]


def rescale(values, factor):
    return values * factor.reshape(factor.shape + (1,) * (values.ndim - factor.ndim))


def fold_pair(first, second):
    best = jnp.maximum(first[0], second[0])
    first_scale = jnp.exp(first[0] - best)
    second_scale = jnp.exp(second[0] - best)
    merged = [
        rescale(left_part, first_scale) + rescale(right_part, second_scale)
        for left_part, right_part in zip(first[1:], second[1:])
    ]
    return (best,) + tuple(merged)


def body(
    single,
    pair,
    frames,
    chain,
    mask,
    w_query,
    w_key_value,
    w_query_points,
    w_kv_points,
    w_pair_bias,
    head_weights,
    chain_bias,
    w_out,
    out_gain,
    w_backbone,
):
    rows = single.shape[0]
    half = pair.shape[2]
    width = pair.shape[3]
    heads_here = w_pair_bias.shape[1]
    head_size = w_query.shape[1] // heads_here
    query_count = w_query_points.shape[1] // (3 * heads_here)
    value_count = w_kv_points.shape[1] // (3 * heads_here) - query_count
    pair_keys = pair.reshape(rows, pair.shape[1] * half, width)
    query = jnp.dot(single, w_query, preferred_element_type=jnp.float32).reshape(
        rows, heads_here, head_size
    )
    query_local = jnp.dot(single, w_query_points, preferred_element_type=jnp.float32)
    query_points = to_global(query_local.reshape(rows, heads_here * query_count, 3), frames)
    query_points = query_points.reshape(rows, heads_here, query_count, 3)
    query_chain = chain.astype(jnp.float32)
    query_present = mask.astype(jnp.float32)
    distance_scale = jax.nn.softplus(head_weights) * math.sqrt(2.0 / (9.0 * query_count)) / 2.0
    position = lax.axis_index("pair")
    key_single = lax.dynamic_slice_in_dim(single, position * half, half, 0)
    key_frames = lax.dynamic_slice_in_dim(frames, position * half, half, 1)
    key_chain = lax.dynamic_slice_in_dim(query_chain, position * half, half, 0)
    key_present = lax.dynamic_slice_in_dim(query_present, position * half, half, 0)
    key_value = jnp.dot(key_single, w_key_value, preferred_element_type=jnp.float32)
    key_local = jnp.dot(key_single, w_kv_points, preferred_element_type=jnp.float32)
    key_global = to_global(
        key_local.reshape(half, heads_here * (query_count + value_count), 3), key_frames
    )
    payload = jnp.concatenate([key_value, key_global.reshape(half, -1)], axis=1)
    key_meta = jnp.stack([key_chain, key_present], axis=1)
    split_at = heads_here * 2 * head_size

    def absorb(carry, moving, moving_meta, start):
        top, total, sum_values, sum_points, sum_pair = carry
        count = moving.shape[0]
        pieces = moving[:, :split_at].reshape(count, heads_here, 2, head_size)
        points = moving[:, split_at:].reshape(count, heads_here, query_count + value_count, 3)
        pair_rows = lax.dynamic_slice_in_dim(pair_keys, start, count, 1)
        logits = attention_logits(
            pair_rows,
            query,
            query_points,
            query_chain,
            query_present,
            pieces[:, :, 0],
            points[:, :, :query_count],
            moving_meta[:, 0],
            moving_meta[:, 1],
            w_pair_bias,
            distance_scale,
            chain_bias,
        )
        new_top = jnp.maximum(top, jnp.max(logits, axis=1))
        scale = jnp.exp(top - new_top)
        weights = jnp.exp(logits - new_top[:, None, :])
        total = total * scale + jnp.sum(weights, axis=1)
        sum_values = sum_values * scale[..., None] + jnp.einsum(
            "ijh,jhc->ihc", weights, pieces[:, :, 1], precision=HIGH
        )
        sum_points = sum_points * scale[..., None, None] + jnp.einsum(
            "ijh,jhpd->ihpd", weights, points[:, :, query_count:], precision=HIGH
        )
        sum_pair = sum_pair * scale[..., None] + jnp.einsum(
            "ijh,ijc->ihc",
            weights.astype(jnp.bfloat16),
            pair_rows,
            preferred_element_type=jnp.float32,
        )
        return (new_top, total, sum_values, sum_points, sum_pair)

    initial = (
        jnp.full((rows, heads_here), -1e30, jnp.float32),
        jnp.zeros((rows, heads_here), jnp.float32),
        jnp.zeros((rows, heads_here, head_size), jnp.float32),
        jnp.zeros((rows, heads_here, value_count, 3), jnp.float32),
        jnp.zeros((rows, heads_here, width), jnp.float32),
    )
    block = lax.axis_index("blk")
    blocks = lax.axis_size("blk")
    carry = absorb(initial, payload, key_meta, block * half)

    def advance(step, state):
        carry, moving, moving_meta = state
        moving, moving_meta = shifted((moving, moving_meta), "blk", 1)
        source = (block - step) % blocks
        return (absorb(carry, moving, moving_meta, source * half), moving, moving_meta)

    carry = lax.fori_loop(1, blocks, advance, (carry, payload, key_meta))[0]
    best, total, sum_values, sum_points, sum_pair = combined_all(carry, "pair", fold_pair)
    attended = sum_values / total[..., None]
    pointed = to_local(sum_points / total[..., None, None], frames)
    point_norms = jnp.sqrt(jnp.sum(pointed * pointed, axis=3) + 1.0)
    paired = sum_pair / total[..., None]
    joined = jnp.concatenate(
        [attended, pointed.reshape(rows, heads_here, value_count * 3), point_norms, paired], axis=2
    ).astype(jnp.bfloat16)
    partial_update = jnp.dot(
        joined.reshape(rows, -1),
        w_out.reshape(-1, w_out.shape[2]),
        preferred_element_type=jnp.float32,
    )
    update = lax.psum(partial_update, "head")
    mixed = single.astype(jnp.float32) + update
    centre = jnp.mean(mixed, axis=1, keepdims=True)
    spread = jnp.mean(jnp.square(mixed - centre), axis=1, keepdims=True)
    single_out = ((mixed - centre) * lax.rsqrt(spread + 1e-05) * out_gain).astype(jnp.bfloat16)
    motion = jnp.dot(single_out, w_backbone, preferred_element_type=jnp.float32)
    frames_new = compose(frames, motion)
    frames_out = lax.all_gather(frames_new, "blk", axis=1, tiled=True)
    return (single_out, frames_out)


def solution(mesh):
    placed = (
        P(("groups", "blk"), None),
        P(("groups", "blk"), None, "pair", None),
        P(None, ("groups", "blk")),
        P(("groups", "blk")),
        P(("groups", "blk")),
        P(None, "head"),
        P(None, "head"),
        P(None, "head"),
        P(None, "head"),
        P(None, "head"),
        P("head"),
        P("head"),
        P("head", None, None),
        P(),
        P(),
    )
    return jax.shard_map(
        body,
        mesh=mesh,
        in_specs=placed,
        out_specs=(P(("groups", "blk"), None), P(None, "groups")),
        check_vma=False,
    )
```

profile of v0, /device:TPU:0, one launch (start us, length us, event | category | flops | bytes accessed | tf_op | source)
XLA Modules:
  0.0 85.5 jit_solution(7720689807309747148)
XLA Ops:
  0.7 0.7 copy-done.13
  2.6 0.6 copy-done.3
  3.1 1.1 %fusion.59 = f32[16,192]{1,0:T(8,128)S(1)} fusion(bf16[384,192]{0,1:T(8,128)(2,1)} %param.23, bf16[32,384]{1,0:T(8,128)(2,1)S(1)} %copy-done.3, s32[]{:T(128)S(6)} %select_n.43), kind=kOutput, calls=%fused_computation.96 | convolution fusion | flops 2359296 | bytes 172036 | tf_op jit(solution)/shard_map/dot_general | solution.py:145
  4.6 0.8 copy-done.7
  6.6 0.7 copy-done.4
  12.0 35.5 %while.7 = (s32[]{:T(128)}, f32[32,6]{0,1:T(8,128)S(1)}, f32[32,6]{0,1:T(8,128)S(1)}, f32[32,6,16]{0,2,1:T(8,128)S(1)}, f32[32,6,8,3]{0,2,3,1:T(8,128)S(1)}, /*i...) while((s32[]{:T(128)}, f32[32,6]{0,1:T(8,128)S(1)}, ...), condition=%wide.region_7.8_spmd, body=%wide.region_3.7_spmd.sunk | while | flops 3855250 | bytes 1648512 | solution.py:209
  12.0 3.1 %collective-permute-start = (f32[16,2]{0,1:T(2,128)S(1)}, f32[16,2]{0,1:T(2,128)S(1)}, u32[]{:S(2)}, u32[]{:S(2)}) collective-permute-start(f32[16,2]{0,1:T(2,128)S(1)} %get-tuple-element.757), channel_id=1, source_target_pairs={{0,4},{4,8},{8,12},{12,0},{1,5},{5,9},{9,13},{13,1},{2,6},{6,10},{... | collective-permute-start | bytes 392 | tf_op jit(solution)/shard_map/while/body/eval_jaxpr/ppermute | solution.py:14
  15.1 1.6 %collective-permute-start.1 = (f32[16,408]{0,1:T(8,128)S(1)}, f32[16,408]{0,1:T(8,128)S(1)}, u32[]{:S(2)}, u32[]{:S(2)}) collective-permute-start(f32[16,408]{0,1:T(8,128)S(1)} %get-tuple-element.756), channel_id=1, source_target_pairs={{0,4},{4,8},{8,12},{12,0},{1,5},{5,9},{9,13},{13,1},{2,6},{6,10},{... | collective-permute-start | bytes 78344 | tf_op jit(solution)/shard_map/while/body/eval_jaxpr/ppermute | solution.py:14
  17.2 1.5 %collective-permute-done = f32[16,2]{0,1:T(2,128)S(1)} collective-permute-done((f32[16,2]{0,1:T(2,128)S(1)}, f32[16,2]{0,1:T(2,128)S(1)}, u32[]{:S(2)}, u32[]{:S(2)}) %collective-permute-start) | collective-permute-done | bytes 160 | tf_op jit(solution)/shard_map/while/body/eval_jaxpr/ppermute | solution.py:14
  18.9 4.7 %collective-permute-done.1 = f32[16,408]{0,1:T(8,128)S(1)} collective-permute-done((f32[16,408]{0,1:T(8,128)S(1)}, f32[16,408]{0,1:T(8,128)S(1)}, u32[]{:S(2)}, u32[]{:S(2)}) %collective-permute-start.1) | collective-permute-done | bytes 26144 | tf_op jit(solution)/shard_map/while/body/eval_jaxpr/ppermute | solution.py:14
  23.7 0.6 copy-done.1
  25.3 0.6 slice-done
  26.5 1.4 %collective-permute-start.1 = (f32[16,408]{0,1:T(8,128)S(1)}, f32[16,408]{0,1:T(8,128)S(1)}, u32[]{:S(2)}, u32[]{:S(2)}) collective-permute-start(f32[16,408]{0,1:T(8,128)S(1)} %get-tuple-element.756), channel_id=1, source_target_pairs={{0,4},{4,8},{8,12},{12,0},{1,5},{5,9},{9,13},{13,1},{2,6},{6,10},{... | collective-permute-start | bytes 78344 | tf_op jit(solution)/shard_map/while/body/eval_jaxpr/ppermute | solution.py:14
  28.3 3.5 %collective-permute-done = f32[16,2]{0,1:T(2,128)S(1)} collective-permute-done((f32[16,2]{0,1:T(2,128)S(1)}, f32[16,2]{0,1:T(2,128)S(1)}, u32[]{:S(2)}, u32[]{:S(2)}) %collective-permute-start) | collective-permute-done | bytes 160 | tf_op jit(solution)/shard_map/while/body/eval_jaxpr/ppermute | solution.py:14
  32.0 2.1 %collective-permute-done.1 = f32[16,408]{0,1:T(8,128)S(1)} collective-permute-done((f32[16,408]{0,1:T(8,128)S(1)}, f32[16,408]{0,1:T(8,128)S(1)}, u32[]{:S(2)}, u32[]{:S(2)}) %collective-permute-start.1) | collective-permute-done | bytes 26144 | tf_op jit(solution)/shard_map/while/body/eval_jaxpr/ppermute | solution.py:14
  34.2 0.6 copy-done.1
  35.9 0.6 slice-done
  37.1 0.6 collective-permute-start.1
  38.2 4.3 %collective-permute-done = f32[16,2]{0,1:T(2,128)S(1)} collective-permute-done((f32[16,2]{0,1:T(2,128)S(1)}, f32[16,2]{0,1:T(2,128)S(1)}, u32[]{:S(2)}, u32[]{:S(2)}) %collective-permute-start) | collective-permute-done | bytes 160 | tf_op jit(solution)/shard_map/while/body/eval_jaxpr/ppermute | solution.py:14
  42.6 2.1 %collective-permute-done.1 = f32[16,408]{0,1:T(8,128)S(1)} collective-permute-done((f32[16,408]{0,1:T(8,128)S(1)}, f32[16,408]{0,1:T(8,128)S(1)}, u32[]{:S(2)}, u32[]{:S(2)}) %collective-permute-start.1) | collective-permute-done | bytes 26144 | tf_op jit(solution)/shard_map/while/body/eval_jaxpr/ppermute | solution.py:14
  44.8 0.6 copy-done.1
  46.4 0.6 slice-done
  47.6 1.8 %all-gather.5 = f32[2,32,6]{1,2,0:T(8,128)S(1)} all-gather(f32[1,32,6]{1,2,0:T(8,128)S(1)} %bitcast.281), channel_id=3, replica_groups=mesh['groups'=2,'blk'=4,'head'=2,'pair'=2] {'pair'}, dimensions={0}, use_global_device_ids=true | all-gather | bytes 2304 | tf_op jit(solution)/shard_map/all_gather | solution.py:18
  49.4 1.8 %all-gather.6 = f32[2,32,6]{1,2,0:T(8,128)S(1)} all-gather(f32[1,32,6]{1,2,0:T(8,128)S(1)} %bitcast.282), channel_id=4, replica_groups=mesh['groups'=2,'blk'=4,'head'=2,'pair'=2] {'pair'}, dimensions={0}, use_global_device_ids=true | all-gather | bytes 2304 | tf_op jit(solution)/shard_map/all_gather | solution.py:18
  51.5 1.9 %all-gather.4 = f32[64,6,128]{2,0,1:T(8,128)S(1)} all-gather(f32[32,6,128]{2,0,1:T(8,128)S(1)} %copy.259), channel_id=6, replica_groups=mesh['groups'=2,'blk'=4,'head'=2,'pair'=2] {'pair'}, dimensions={0}, use_global_device_ids=true | all-gather | bytes 294912 | tf_op jit(solution)/shard_map/all_gather | solution.py:18
  53.7 1.9 %all-gather = f32[64,6,16]{2,0,1:T(8,128)S(1)} all-gather(f32[32,6,16]{2,0,1:T(8,128)S(1)} %copy.249), channel_id=2, replica_groups=mesh['groups'=2,'blk'=4,'head'=2,'pair'=2] {'pair'}, dimensions={0}, use_global_device_ids=true | all-gather | bytes 36864 | tf_op jit(solution)/shard_map/all_gather | solution.py:18
  56.0 2.4 %all-gather.3 = f32[64,6,8,3]{2,1,3,0:T(8,128)S(1)} all-gather(f32[32,6,8,3]{2,1,3,0:T(8,128)S(1)} %copy.250), channel_id=5, replica_groups=mesh['groups'=2,'blk'=4,'head'=2,'pair'=2] {'pair'}, dimensions={0}, use_global_device_ids=true | all-gather | bytes 55296 | tf_op jit(solution)/shard_map/all_gather | solution.py:18
  58.6 1.1 %fusion.82 = (bf16[32,6,8,3]{2,3,1,0:T(4,128)(2,1)S(1)}, f32[32,6,8]{2,1,0:T(8,128)S(1)}) fusion(f32[3,3,32,1]{0,1,3,2:T(4,128)S(1)} %copy.271, f32[32,6,8,3]{2,1,3,0:T(8,128)S(1)} %fusion.30), kind=kOutput, calls=%fused_computation.152 | convolution fusion | flops 178176 | bytes 34944 | tf_op jit(solution)/shard_map/abn,nhpa->nhpb/dot_general | solution.py:34
  60.7 8.6 %psum.7 = f32[32,384]{1,0:T(8,128)S(1)} all-reduce(f32[32,384]{1,0:T(8,128)S(1)} %convolution_bitcast_fusion.4), channel_id=1, replica_groups=mesh['groups'=2,'blk'=4,'head'=2,'pair'=2] {'head'}, use_global_device_ids=true, to_apply=%region_9.10 | all-reduce | flops 12288 | bytes 98304 | tf_op jit(solution)/shard_map/psum | solution.py:223
  69.7 0.6 copy-done.11
  71.6 13.1 %all-gather.7 = f32[4,32,12]{1,2,0:T(8,128)S(1)} all-gather(f32[1,32,12]{1,2,0:T(8,128)S(1)} %maximum_bitcast_fusion), channel_id=1, replica_groups=mesh['groups'=2,'blk'=4,'head'=2,'pair'=2] {'blk'}, dimensions={0}, use_global_device_ids=true | all-gather | bytes 7680 | tf_op jit(solution)/shard_map/all_gather | solution.py:230
  84.8 0.7 reshape.714
  (192 shorter events, 17.7 us)
Async XLA Ops:
  0.6 59.6 %copy-start = (bf16[6,176,384]{2,1,0:T(8,128)(2,1)S(1)}, bf16[6,176,384]{2,1,0:T(8,128)(2,1)}, u32[]{:S(2)}) copy-start(bf16[6,176,384]{2,1,0:T(8,128)(2,1)} %param.29) | copy-start | bytes 2433028
  0.7 0.7 copy-start.13
  0.7 0.7 copy-start.14
  0.7 0.7 copy-start.15
  1.4 0.7 copy-start.8
  2.4 0.7 copy-start.3
  3.1 1.2 %copy-start.9 = (bf16[384,72]{0,1:T(8,128)(2,1)S(1)}, bf16[384,72]{0,1:T(8,128)(2,1)}, u32[]{:S(2)}) copy-start(bf16[384,72]{0,1:T(8,128)(2,1)} %param.24) | copy-start | bytes 165892
  4.5 0.9 %copy-start.7 = (bf16[384,96]{0,1:T(8,128)(2,1)S(1)}, bf16[384,96]{0,1:T(8,128)(2,1)}, u32[]{:S(2)}) copy-start(bf16[384,96]{0,1:T(8,128)(2,1)} %param.22) | copy-start | bytes 221188
  6.5 0.9 %copy-start.4 = (bf16[384,216]{0,1:T(8,128)(2,1)S(1)}, bf16[384,216]{0,1:T(8,128)(2,1)}, u32[]{:S(2)}) copy-start(bf16[384,216]{0,1:T(8,128)(2,1)} %param.25) | copy-start | bytes 497668
  7.6 1.0 %copy-start.2 = (bf16[32,4,16,128]{3,2,1,0:T(8,128)(2,1)S(1)}, bf16[32,4,16,128]{3,2,1,0:T(8,128)(2,1)}, u32[]{:S(2)}) copy-start(bf16[32,4,16,128]{3,2,1,0:T(8,128)(2,1)} %param.18) | copy-start | bytes 1572868
  8.3 0.7 copy-start.6
  9.8 0.7 copy-start.10
  12.0 6.7 %collective-permute-start = (f32[16,2]{0,1:T(2,128)S(1)}, f32[16,2]{0,1:T(2,128)S(1)}, u32[]{:S(2)}, u32[]{:S(2)}) collective-permute-start(f32[16,2]{0,1:T(2,128)S(1)} %get-tuple-element.757), channel_id=1, source_target_pairs={{0,4},{4,8},{8,12},{12,0},{1,5},{5,9},{9,13},{13,1},{2,6},{6,10},{... | collective-permute-start | bytes 392 | tf_op jit(solution)/shard_map/while/body/eval_jaxpr/ppermute | solution.py:14
  15.1 8.4 %collective-permute-start.1 = (f32[16,408]{0,1:T(8,128)S(1)}, f32[16,408]{0,1:T(8,128)S(1)}, u32[]{:S(2)}, u32[]{:S(2)}) collective-permute-start(f32[16,408]{0,1:T(8,128)S(1)} %get-tuple-element.756), channel_id=1, source_target_pairs={{0,4},{4,8},{8,12},{12,0},{1,5},{5,9},{9,13},{13,1},{2,6},{6,10},{... | collective-permute-start | bytes 78344 | tf_op jit(solution)/shard_map/while/body/eval_jaxpr/ppermute | solution.py:14
  23.6 0.7 copy-start.1
  25.0 0.9 %slice-start = ((f32[16,6,12,3]{0,3,2,1:T(4,128)}), f32[16,6,8,3]{0,3,2,1:T(4,128)S(1)}, s32[]{:S(2)}) async-start(f32[16,6,12,3]{0,3,2,1:T(4,128)} %copy-done.1), calls=%async_computation | async-start | bytes 196608 | tf_op jit(solution)/shard_map/while/body/eval_jaxpr/slice | solution.py:182
  26.4 5.4 %collective-permute-start = (f32[16,2]{0,1:T(2,128)S(1)}, f32[16,2]{0,1:T(2,128)S(1)}, u32[]{:S(2)}, u32[]{:S(2)}) collective-permute-start(f32[16,2]{0,1:T(2,128)S(1)} %get-tuple-element.757), channel_id=1, source_target_pairs={{0,4},{4,8},{8,12},{12,0},{1,5},{5,9},{9,13},{13,1},{2,6},{6,10},{... | collective-permute-start | bytes 392 | tf_op jit(solution)/shard_map/while/body/eval_jaxpr/ppermute | solution.py:14
  26.5 7.7 %collective-permute-start.1 = (f32[16,408]{0,1:T(8,128)S(1)}, f32[16,408]{0,1:T(8,128)S(1)}, u32[]{:S(2)}, u32[]{:S(2)}) collective-permute-start(f32[16,408]{0,1:T(8,128)S(1)} %get-tuple-element.756), channel_id=1, source_target_pairs={{0,4},{4,8},{8,12},{12,0},{1,5},{5,9},{9,13},{13,1},{2,6},{6,10},{... | collective-permute-start | bytes 78344 | tf_op jit(solution)/shard_map/while/body/eval_jaxpr/ppermute | solution.py:14
  34.2 0.7 copy-start.1
  35.6 0.9 %slice-start = ((f32[16,6,12,3]{0,3,2,1:T(4,128)}), f32[16,6,8,3]{0,3,2,1:T(4,128)S(1)}, s32[]{:S(2)}) async-start(f32[16,6,12,3]{0,3,2,1:T(4,128)} %copy-done.1), calls=%async_computation | async-start | bytes 196608 | tf_op jit(solution)/shard_map/while/body/eval_jaxpr/slice | solution.py:182
  37.0 5.4 %collective-permute-start = (f32[16,2]{0,1:T(2,128)S(1)}, f32[16,2]{0,1:T(2,128)S(1)}, u32[]{:S(2)}, u32[]{:S(2)}) collective-permute-start(f32[16,2]{0,1:T(2,128)S(1)} %get-tuple-element.757), channel_id=1, source_target_pairs={{0,4},{4,8},{8,12},{12,0},{1,5},{5,9},{9,13},{13,1},{2,6},{6,10},{... | collective-permute-start | bytes 392 | tf_op jit(solution)/shard_map/while/body/eval_jaxpr/ppermute | solution.py:14
  37.1 7.7 %collective-permute-start.1 = (f32[16,408]{0,1:T(8,128)S(1)}, f32[16,408]{0,1:T(8,128)S(1)}, u32[]{:S(2)}, u32[]{:S(2)}) collective-permute-start(f32[16,408]{0,1:T(8,128)S(1)} %get-tuple-element.756), channel_id=1, source_target_pairs={{0,4},{4,8},{8,12},{12,0},{1,5},{5,9},{9,13},{13,1},{2,6},{6,10},{... | collective-permute-start | bytes 78344 | tf_op jit(solution)/shard_map/while/body/eval_jaxpr/ppermute | solution.py:14
  44.8 0.7 copy-start.1
  46.1 0.9 %slice-start = ((f32[16,6,12,3]{0,3,2,1:T(4,128)}), f32[16,6,8,3]{0,3,2,1:T(4,128)S(1)}, s32[]{:S(2)}) async-start(f32[16,6,12,3]{0,3,2,1:T(4,128)} %copy-done.1), calls=%async_computation | async-start | bytes 196608 | tf_op jit(solution)/shard_map/while/body/eval_jaxpr/slice | solution.py:182
  60.3 9.3 %copy-start.12 = (f32[384]{0:T(512)S(1)}, f32[384]{0:T(512)}, u32[]{:S(2)}) copy-start(f32[384]{0:T(512)} %param.30) | copy-start | bytes 4612
  69.6 0.7 copy-start.11
  70.3 0.6 copy-start.5
where the time goes:
time: 86 us; the launch traced here: 85.5 us
  blocking collectives  31.6 us (37%)
  waiting for transfers between devices  18.2 us (21%)
  local copies, waits for them, and re-layouts  15 us (17%)
  matrix products  9.58 us (11%)
  starting transfers between devices  6.74 us (8%)
  other arithmetic  2.83 us (3%)
  between operations  1.1 us (1%)
    ppermute x6, waiting for transfers between devices, shifted(): lax.ppermute(array, axis, [(i, (i + by) % peers) for i in range(peers)])  18.2 us
    all_gather x1, blocking collectives, body(): frames_out = lax.all_gather(frames_new, 'blk', axis=1, tiled=True)  13.1 us
    all_gather x5, blocking collectives, combined_all(): pieces = jax.tree.map(lambda part: lax.all_gather(part, axis), value)  9.88 us
    psum x1, blocking collectives, body(): update = lax.psum(partial_update, 'head')  8.59 us
    ppermute x6, starting transfers between devices, shifted(): lax.ppermute(array, axis, [(i, (i + by) % peers) for i in range(peers)])  6.74 us
    unnamed x32, local copies, waits for them, and re-layouts  6.07 us
    while x15, local copies, waits for them, and re-layouts  1.94 us
    slice x7, local copies, waits for them, and re-layouts, absorb(): points[:, :, query_count:]  1.86 us
  transfers between devices with their start and end apart: 6, of which 6 were waited for; matrix products, arithmetic and copies ran while one was open for 2% of the time, Pallas kernels for 0%

commit v1 on v0

--- a/solution.py
+++ b/solution.py
@@ -227,7 +227,12 @@
     single_out = ((mixed - centre) * lax.rsqrt(spread + 1e-05) * out_gain).astype(jnp.bfloat16)
     motion = jnp.dot(single_out, w_backbone, preferred_element_type=jnp.float32)
     frames_new = compose(frames, motion)
-    frames_out = lax.all_gather(frames_new, "blk", axis=1, tiled=True)
+    ring = [frames_new]
+    for hop in range(3):
+        ring.append(lax.ppermute(ring[-1], "blk", [(dev, (dev + 1) % 4) for dev in range(4)]))
+    frames_out = jnp.roll(
+        jnp.concatenate(ring[::-1], axis=1), (lax.axis_index("blk") + 1) * ring[0].shape[1], axis=1
+    )
     return (single_out, frames_out)
 
 

time: 86 us -> 90.1 us (1.048)
  waiting for transfers between devices: 18.2 us -> 34.6 us
  blocking collectives: 31.6 us -> 18.5 us
    ppermute x0 -> x3, waiting for transfers between devices: none -> 16.3 us  [body(): lax.ppermute(ring[-1], 'blk', [(dev, (dev + 1) % 4) for dev in range(4)])]
    all_gather x1 -> x0, blocking collectives: 13.1 us -> none  [body(): frames_out = lax.all_gather(frames_new, 'blk', axis=1, tiled=True)]
    dot_general x1, matrix products: 1.06 us -> 0.16 us  [body(): jnp.dot(key_single, w_key_value, preferred_element_type=jnp.float32)]
    unnamed x32 -> x31, local copies, waits for them, and re-layouts: 6.07 us -> 6.22 us
  transfers between devices with their start and end apart: 6 -> 9, of which waited for: 6 -> 9; matrix products, arithmetic and copies ran while one was open for 2% -> 2% of each run, Pallas kernels for 0% -> 0%
where the time goes in v1:
time: 90.1 us; the launch traced here: 89.5 us
  waiting for transfers between devices  34.6 us (38%)
  blocking collectives  18.5 us (21%)
  local copies, waits for them, and re-layouts  15.9 us (18%)
  matrix products  9.48 us (11%)
  starting transfers between devices  6.79 us (8%)
  other arithmetic  2.83 us (3%)
  between operations  1.11 us (1%)
    ppermute x6, waiting for transfers between devices, shifted(): lax.ppermute(array, axis, [(i, (i + by) % peers) for i in range(peers)])  18.2 us
    ppermute x3, waiting for transfers between devices, body(): lax.ppermute(ring[-1], 'blk', [(dev, (dev + 1) % 4) for dev in range(4)])  16.3 us
    all_gather x5, blocking collectives, combined_all(): pieces = jax.tree.map(lambda part: lax.all_gather(part, axis), value)  9.88 us
    psum x1, blocking collectives, body(): update = lax.psum(partial_update, 'head')  8.6 us
    ppermute x6, starting transfers between devices, shifted(): lax.ppermute(array, axis, [(i, (i + by) % peers) for i in range(peers)])  6.72 us
    unnamed x31, local copies, waits for them, and re-layouts  6.22 us
    while x15, local copies, waits for them, and re-layouts  1.94 us
    slice x7, local copies, waits for them, and re-layouts, absorb(): points[:, :, query_count:]  1.86 us
  transfers between devices with their start and end apart: 9, of which 9 were waited for; matrix products, arithmetic and copies ran while one was open for 2% of the time, Pallas kernels for 0%

profile of v1, /device:TPU:0, one launch (start us, length us, event | category | flops | bytes accessed | tf_op | source)
XLA Modules:
  0.0 89.5 jit_solution(17439933111564739573)
XLA Ops:
  0.7 0.7 copy-done.13
  3.0 1.0 %fusion.86 = f32[32,72]{0,1:T(8,128)S(1)} fusion(bf16[32,384]{1,0:T(8,128)(2,1)S(1)} %copy-done.3, bf16[384,72]{0,1:T(8,128)(2,1)} %param.24), kind=kOutput, calls=%fused_computation.157 | convolution fusion | flops 1769472 | bytes 89088 | tf_op jit(solution)/shard_map/dot_general | solution.py:134
  6.3 0.6 copy-done.15
  7.2 0.7 copy-done.8
  10.7 0.6 copy-done.10
  12.8 35.5 %while.7 = (s32[]{:T(128)}, f32[32,6]{0,1:T(8,128)S(1)}, f32[32,6]{0,1:T(8,128)S(1)}, f32[32,6,16]{0,2,1:T(8,128)S(1)}, f32[32,6,8,3]{0,2,3,1:T(8,128)S(1)}, /*i...) while((s32[]{:T(128)}, f32[32,6]{0,1:T(8,128)S(1)}, ...), condition=%wide.region_7.8_spmd, body=%wide.region_3.7_spmd.sunk | while | flops 3855250 | bytes 1648512 | solution.py:209
  12.8 3.1 %collective-permute-start = (f32[16,2]{0,1:T(2,128)S(1)}, f32[16,2]{0,1:T(2,128)S(1)}, u32[]{:S(2)}, u32[]{:S(2)}) collective-permute-start(f32[16,2]{0,1:T(2,128)S(1)} %get-tuple-element.740), channel_id=1, source_target_pairs={{0,4},{4,8},{8,12},{12,0},{1,5},{5,9},{9,13},{13,1},{2,6},{6,10},{... | collective-permute-start | bytes 392 | tf_op jit(solution)/shard_map/while/body/eval_jaxpr/ppermute | solution.py:14
  15.9 1.6 %collective-permute-start.1 = (f32[16,408]{0,1:T(8,128)S(1)}, f32[16,408]{0,1:T(8,128)S(1)}, u32[]{:S(2)}, u32[]{:S(2)}) collective-permute-start(f32[16,408]{0,1:T(8,128)S(1)} %get-tuple-element.739), channel_id=1, source_target_pairs={{0,4},{4,8},{8,12},{12,0},{1,5},{5,9},{9,13},{13,1},{2,6},{6,10},{... | collective-permute-start | bytes 78344 | tf_op jit(solution)/shard_map/while/body/eval_jaxpr/ppermute | solution.py:14
  18.0 1.5 %collective-permute-done = f32[16,2]{0,1:T(2,128)S(1)} collective-permute-done((f32[16,2]{0,1:T(2,128)S(1)}, f32[16,2]{0,1:T(2,128)S(1)}, u32[]{:S(2)}, u32[]{:S(2)}) %collective-permute-start) | collective-permute-done | bytes 160 | tf_op jit(solution)/shard_map/while/body/eval_jaxpr/ppermute | solution.py:14
  19.6 4.7 %collective-permute-done.1 = f32[16,408]{0,1:T(8,128)S(1)} collective-permute-done((f32[16,408]{0,1:T(8,128)S(1)}, f32[16,408]{0,1:T(8,128)S(1)}, u32[]{:S(2)}, u32[]{:S(2)}) %collective-permute-start.1) | collective-permute-done | bytes 26144 | tf_op jit(solution)/shard_map/while/body/eval_jaxpr/ppermute | solution.py:14
  24.4 0.6 copy-done.1
  27.2 1.3 %collective-permute-start.1 = (f32[16,408]{0,1:T(8,128)S(1)}, f32[16,408]{0,1:T(8,128)S(1)}, u32[]{:S(2)}, u32[]{:S(2)}) collective-permute-start(f32[16,408]{0,1:T(8,128)S(1)} %get-tuple-element.739), channel_id=1, source_target_pairs={{0,4},{4,8},{8,12},{12,0},{1,5},{5,9},{9,13},{13,1},{2,6},{6,10},{... | collective-permute-start | bytes 78344 | tf_op jit(solution)/shard_map/while/body/eval_jaxpr/ppermute | solution.py:14
  29.1 3.5 %collective-permute-done = f32[16,2]{0,1:T(2,128)S(1)} collective-permute-done((f32[16,2]{0,1:T(2,128)S(1)}, f32[16,2]{0,1:T(2,128)S(1)}, u32[]{:S(2)}, u32[]{:S(2)}) %collective-permute-start) | collective-permute-done | bytes 160 | tf_op jit(solution)/shard_map/while/body/eval_jaxpr/ppermute | solution.py:14
  32.8 2.1 %collective-permute-done.1 = f32[16,408]{0,1:T(8,128)S(1)} collective-permute-done((f32[16,408]{0,1:T(8,128)S(1)}, f32[16,408]{0,1:T(8,128)S(1)}, u32[]{:S(2)}, u32[]{:S(2)}) %collective-permute-start.1) | collective-permute-done | bytes 26144 | tf_op jit(solution)/shard_map/while/body/eval_jaxpr/ppermute | solution.py:14
  35.0 0.6 copy-done.1
  37.8 0.6 collective-permute-start.1
  38.9 4.2 %collective-permute-done = f32[16,2]{0,1:T(2,128)S(1)} collective-permute-done((f32[16,2]{0,1:T(2,128)S(1)}, f32[16,2]{0,1:T(2,128)S(1)}, u32[]{:S(2)}, u32[]{:S(2)}) %collective-permute-start) | collective-permute-done | bytes 160 | tf_op jit(solution)/shard_map/while/body/eval_jaxpr/ppermute | solution.py:14
  43.3 2.1 %collective-permute-done.1 = f32[16,408]{0,1:T(8,128)S(1)} collective-permute-done((f32[16,408]{0,1:T(8,128)S(1)}, f32[16,408]{0,1:T(8,128)S(1)}, u32[]{:S(2)}, u32[]{:S(2)}) %collective-permute-start.1) | collective-permute-done | bytes 26144 | tf_op jit(solution)/shard_map/while/body/eval_jaxpr/ppermute | solution.py:14
  45.6 0.6 copy-done.1
  47.2 0.6 slice-done
  48.4 1.8 %all-gather.5 = f32[2,32,6]{1,2,0:T(8,128)S(1)} all-gather(f32[1,32,6]{1,2,0:T(8,128)S(1)} %bitcast.274), channel_id=3, replica_groups=mesh['groups'=2,'blk'=4,'head'=2,'pair'=2] {'pair'}, dimensions={0}, use_global_device_ids=true | all-gather | bytes 2304 | tf_op jit(solution)/shard_map/all_gather | solution.py:18
  50.2 1.8 %all-gather.6 = f32[2,32,6]{1,2,0:T(8,128)S(1)} all-gather(f32[1,32,6]{1,2,0:T(8,128)S(1)} %bitcast.275), channel_id=4, replica_groups=mesh['groups'=2,'blk'=4,'head'=2,'pair'=2] {'pair'}, dimensions={0}, use_global_device_ids=true | all-gather | bytes 2304 | tf_op jit(solution)/shard_map/all_gather | solution.py:18
  52.3 1.9 %all-gather.4 = f32[64,6,128]{2,0,1:T(8,128)S(1)} all-gather(f32[32,6,128]{2,0,1:T(8,128)S(1)} %copy.216), channel_id=6, replica_groups=mesh['groups'=2,'blk'=4,'head'=2,'pair'=2] {'pair'}, dimensions={0}, use_global_device_ids=true | all-gather | bytes 294912 | tf_op jit(solution)/shard_map/all_gather | solution.py:18
  54.4 1.9 %all-gather = f32[64,6,16]{2,0,1:T(8,128)S(1)} all-gather(f32[32,6,16]{2,0,1:T(8,128)S(1)} %copy.206), channel_id=2, replica_groups=mesh['groups'=2,'blk'=4,'head'=2,'pair'=2] {'pair'}, dimensions={0}, use_global_device_ids=true | all-gather | bytes 36864 | tf_op jit(solution)/shard_map/all_gather | solution.py:18
  56.7 2.4 %all-gather.3 = f32[64,6,8,3]{2,1,3,0:T(8,128)S(1)} all-gather(f32[32,6,8,3]{2,1,3,0:T(8,128)S(1)} %copy.207), channel_id=5, replica_groups=mesh['groups'=2,'blk'=4,'head'=2,'pair'=2] {'pair'}, dimensions={0}, use_global_device_ids=true | all-gather | bytes 55296 | tf_op jit(solution)/shard_map/all_gather | solution.py:18
  59.4 1.1 %fusion.82 = (bf16[32,6,8,3]{2,3,1,0:T(4,128)(2,1)S(1)}, f32[32,6,8]{2,1,0:T(8,128)S(1)}) fusion(f32[3,3,32,1]{0,1,3,2:T(4,128)S(1)} %copy.227, f32[32,6,8,3]{2,1,3,0:T(8,128)S(1)} %fusion.30), kind=kOutput, calls=%fused_computation.153 | convolution fusion | flops 178176 | bytes 34944 | tf_op jit(solution)/shard_map/abn,nhpa->nhpb/dot_general | solution.py:34
  61.4 8.6 %psum.7 = f32[32,384]{1,0:T(8,128)S(1)} all-reduce(f32[32,384]{1,0:T(8,128)S(1)} %convolution_bitcast_fusion.4), channel_id=1, replica_groups=mesh['groups'=2,'blk'=4,'head'=2,'pair'=2] {'head'}, use_global_device_ids=true, to_apply=%region_9.10 | all-reduce | flops 12288 | bytes 98304 | tf_op jit(solution)/shard_map/psum | solution.py:223
  70.5 0.6 copy-done.11
  72.4 5.4 %collective-permute-done.2 = f32[12,32]{1,0:T(8,128)S(1)} collective-permute-done((f32[12,32]{1,0:T(8,128)S(1)}, f32[12,32]{1,0:T(8,128)S(1)}, u32[]{:S(2)}, u32[]{:S(2)}) %collective-permute-start.2) | collective-permute-done | bytes 1568 | tf_op jit(solution)/shard_map/ppermute | solution.py:232
  77.9 5.4 %collective-permute-done.3 = f32[12,32]{1,0:T(8,128)S(1)} collective-permute-done((f32[12,32]{1,0:T(8,128)S(1)}, f32[12,32]{1,0:T(8,128)S(1)}, u32[]{:S(2)}, u32[]{:S(2)}) %collective-permute-start.3) | collective-permute-done | bytes 1568 | tf_op jit(solution)/shard_map/ppermute | solution.py:232
  83.3 5.4 %collective-permute-done.4 = f32[12,32]{1,0:T(8,128)S(1)} collective-permute-done((f32[12,32]{1,0:T(8,128)S(1)}, f32[12,32]{1,0:T(8,128)S(1)}, u32[]{:S(2)}, u32[]{:S(2)}) %collective-permute-start.4) | collective-permute-done | bytes 1568 | tf_op jit(solution)/shard_map/ppermute | solution.py:232
  88.8 0.7 constant_dynamic-slice_fusion.1
  (197 shorter events, 19.9 us)
Async XLA Ops:
  0.6 60.4 %copy-start = (bf16[6,176,384]{2,1,0:T(8,128)(2,1)S(1)}, bf16[6,176,384]{2,1,0:T(8,128)(2,1)}, u32[]{:S(2)}) copy-start(bf16[6,176,384]{2,1,0:T(8,128)(2,1)} %param.29) | copy-start | bytes 2433028
  0.7 0.7 copy-start.13
  0.7 1.6 %copy-start.9 = (f32[12,32]{1,0:T(8,128)S(1)}, f32[12,32]{1,0:T(8,128)}, u32[]{:S(2)}) copy-start(f32[12,32]{1,0:T(8,128)} %param.19) | copy-start | bytes 4612
  1.5 0.7 copy-start.14
  2.3 0.7 copy-start.3
  4.6 0.9 %copy-start.4 = (bf16[384,216]{0,1:T(8,128)(2,1)S(1)}, bf16[384,216]{0,1:T(8,128)(2,1)}, u32[]{:S(2)}) copy-start(bf16[384,216]{0,1:T(8,128)(2,1)} %param.25) | copy-start | bytes 497668
  6.1 1.0 %copy-start.5 = (bf16[384,192]{0,1:T(8,128)(2,1)S(1)}, bf16[384,192]{0,1:T(8,128)(2,1)}, u32[]{:S(2)}) copy-start(bf16[384,192]{0,1:T(8,128)(2,1)} %param.23) | copy-start | bytes 442372
  6.3 0.7 copy-start.15
  7.1 0.9 %copy-start.8 = (bf16[384,96]{0,1:T(8,128)(2,1)S(1)}, bf16[384,96]{0,1:T(8,128)(2,1)}, u32[]{:S(2)}) copy-start(bf16[384,96]{0,1:T(8,128)(2,1)} %param.22) | copy-start | bytes 221188
  8.1 1.1 %copy-start.2 = (bf16[32,4,16,128]{3,2,1,0:T(8,128)(2,1)S(1)}, bf16[32,4,16,128]{3,2,1,0:T(8,128)(2,1)}, u32[]{:S(2)}) copy-start(bf16[32,4,16,128]{3,2,1,0:T(8,128)(2,1)} %param.18) | copy-start | bytes 1572868
  8.8 0.7 copy-start.7
  10.7 0.7 copy-start.10
  12.8 6.7 %collective-permute-start = (f32[16,2]{0,1:T(2,128)S(1)}, f32[16,2]{0,1:T(2,128)S(1)}, u32[]{:S(2)}, u32[]{:S(2)}) collective-permute-start(f32[16,2]{0,1:T(2,128)S(1)} %get-tuple-element.740), channel_id=1, source_target_pairs={{0,4},{4,8},{8,12},{12,0},{1,5},{5,9},{9,13},{13,1},{2,6},{6,10},{... | collective-permute-start | bytes 392 | tf_op jit(solution)/shard_map/while/body/eval_jaxpr/ppermute | solution.py:14
  15.9 8.4 %collective-permute-start.1 = (f32[16,408]{0,1:T(8,128)S(1)}, f32[16,408]{0,1:T(8,128)S(1)}, u32[]{:S(2)}, u32[]{:S(2)}) collective-permute-start(f32[16,408]{0,1:T(8,128)S(1)} %get-tuple-element.739), channel_id=1, source_target_pairs={{0,4},{4,8},{8,12},{12,0},{1,5},{5,9},{9,13},{13,1},{2,6},{6,10},{... | collective-permute-start | bytes 78344 | tf_op jit(solution)/shard_map/while/body/eval_jaxpr/ppermute | solution.py:14
  24.4 0.7 copy-start.1
  25.7 0.9 slice-start
  27.2 5.4 %collective-permute-start = (f32[16,2]{0,1:T(2,128)S(1)}, f32[16,2]{0,1:T(2,128)S(1)}, u32[]{:S(2)}, u32[]{:S(2)}) collective-permute-start(f32[16,2]{0,1:T(2,128)S(1)} %get-tuple-element.740), channel_id=1, source_target_pairs={{0,4},{4,8},{8,12},{12,0},{1,5},{5,9},{9,13},{13,1},{2,6},{6,10},{... | collective-permute-start | bytes 392 | tf_op jit(solution)/shard_map/while/body/eval_jaxpr/ppermute | solution.py:14
  27.2 7.7 %collective-permute-start.1 = (f32[16,408]{0,1:T(8,128)S(1)}, f32[16,408]{0,1:T(8,128)S(1)}, u32[]{:S(2)}, u32[]{:S(2)}) collective-permute-start(f32[16,408]{0,1:T(8,128)S(1)} %get-tuple-element.739), channel_id=1, source_target_pairs={{0,4},{4,8},{8,12},{12,0},{1,5},{5,9},{9,13},{13,1},{2,6},{6,10},{... | collective-permute-start | bytes 78344 | tf_op jit(solution)/shard_map/while/body/eval_jaxpr/ppermute | solution.py:14
  35.0 0.7 copy-start.1
  36.3 0.9 slice-start
  37.8 5.4 %collective-permute-start = (f32[16,2]{0,1:T(2,128)S(1)}, f32[16,2]{0,1:T(2,128)S(1)}, u32[]{:S(2)}, u32[]{:S(2)}) collective-permute-start(f32[16,2]{0,1:T(2,128)S(1)} %get-tuple-element.740), channel_id=1, source_target_pairs={{0,4},{4,8},{8,12},{12,0},{1,5},{5,9},{9,13},{13,1},{2,6},{6,10},{... | collective-permute-start | bytes 392 | tf_op jit(solution)/shard_map/while/body/eval_jaxpr/ppermute | solution.py:14
  37.8 7.7 %collective-permute-start.1 = (f32[16,408]{0,1:T(8,128)S(1)}, f32[16,408]{0,1:T(8,128)S(1)}, u32[]{:S(2)}, u32[]{:S(2)}) collective-permute-start(f32[16,408]{0,1:T(8,128)S(1)} %get-tuple-element.739), channel_id=1, source_target_pairs={{0,4},{4,8},{8,12},{12,0},{1,5},{5,9},{9,13},{13,1},{2,6},{6,10},{... | collective-permute-start | bytes 78344 | tf_op jit(solution)/shard_map/while/body/eval_jaxpr/ppermute | solution.py:14
  45.5 0.7 copy-start.1
  46.9 0.9 slice-start
  61.0 9.3 %copy-start.12 = (f32[384]{0:T(512)S(1)}, f32[384]{0:T(512)}, u32[]{:S(2)}) copy-start(f32[384]{0:T(512)} %param.30) | copy-start | bytes 4612
  70.4 0.7 copy-start.11
  71.1 0.6 copy-start.6
  72.4 5.5 %collective-permute-start.2 = (f32[12,32]{1,0:T(8,128)S(1)}, f32[12,32]{1,0:T(8,128)S(1)}, u32[]{:S(2)}, u32[]{:S(2)}) collective-permute-start(f32[12,32]{1,0:T(8,128)S(1)} %pad_maximum_fusion.1), channel_id=1, source_target_pairs={{0,4},{4,8},{8,12},{12,0},{1,5},{5,9},{9,13},{13,1},{2,6},{6,10},{... | collective-permute-start | bytes 4616 | tf_op jit(solution)/shard_map/ppermute | solution.py:232
  77.9 5.4 %collective-permute-start.3 = (f32[12,32]{1,0:T(8,128)S(1)}, f32[12,32]{1,0:T(8,128)S(1)}, u32[]{:S(2)}, u32[]{:S(2)}) collective-permute-start(f32[12,32]{1,0:T(8,128)S(1)} %collective-permute-done.2), channel_id=1, source_target_pairs={{0,4},{4,8},{8,12},{12,0},{1,5},{5,9},{9,13},{13,1},{2,6},{6,10},{... | collective-permute-start | bytes 4616 | tf_op jit(solution)/shard_map/ppermute | solution.py:232
  83.3 5.4 %collective-permute-start.4 = (f32[12,32]{1,0:T(8,128)S(1)}, f32[12,32]{1,0:T(8,128)S(1)}, u32[]{:S(2)}, u32[]{:S(2)}) collective-permute-start(f32[12,32]{1,0:T(8,128)S(1)} %collective-permute-done.3), channel_id=1, source_target_pairs={{0,4},{4,8},{8,12},{12,0},{1,5},{5,9},{9,13},{13,1},{2,6},{6,10},{... | collective-permute-start | bytes 4616 | tf_op jit(solution)/shard_map/ppermute | solution.py:232
